TPU v7x, 32 devices: a whole 2x2x4 slice. The times are simulated.
32 devices in a mesh: pack: 16 (over z, x, core), head: 2 (over y), rep: 1.
Axes of the slice: x: 2, y: 2, z: 4, core: 2. Of those that a mesh axis runs over, the one named last changes fastest.
Arguments:
- tokens: bfloat16 [49152, 1024], P(('rep', 'pack')), may hold values from -12 to 12
- ln_gain: float32 [1024], replicated, may hold values from 0.5 to 2
- attn_weight: bfloat16 [1024, 3, 1024], P(None, None, 'head'), may hold values from -6 to 6
- attn_proj: bfloat16 [1024, 1024], P('head'), may hold values from -0.1875 to 0.1875
- page_gain: float32 [1024], replicated, may hold values from 0.5 to 2
- page_weight: bfloat16 [1024, 3, 1024], P(None, None, 'head'), may hold values from -6 to 6
- page_proj: bfloat16 [1024, 1024], P('head'), may hold values from -0.1875 to 0.1875
- page_windows: int32 [48], P('rep'), may hold values from 1 to 12, 192 in all
- page_width: int32 [48], P('rep'), may hold values from 1 to 3
- doc_pages: int32 [12], P('rep'), may hold values from 1 to 8, 48 in all
Outputs:
- mixed: bfloat16 [49152, 1024], P(('rep', 'pack'), 'head')
- page_out: float32 [48, 1024], P('rep', 'head')
Inputs may be any that keep to these rules, and one draw needn't show every extreme that they name: `page_windows`: the pages fill all 192 windows, and one page has exactly 12. `page_width`: A page's last row of windows may be short. `doc_pages`: the documents hold all 48 pages, and one has exactly 8.
All inputs are finite; a program needn't handle non-finite values.
Results may differ from a plain program's by a relative error of at most 0.03.
The roundings to bfloat16 on the way count: a program that leaves them out, or rounds other values in their place, can miss the bound.
Values may be sent and summed in bfloat16 or wider, within the bound.
A program may use at most 128 MiB of HBM per device.

v0:
```python
import math

import jax
import jax.numpy as jnp
from jax import lax
from jax.sharding import PartitionSpec as P

D = 1024
HDIM = 32
WIN = 16
HALO = 4
HALO_WIN = 4


EPS = 1e-05
OFFSETS = ((-1, -1), (-1, 0), (-1, 1), (0, -1), (0, 0), (0, 1), (1, -1), (1, 0), (1, 1))


def with_halo(cells, sides, width):
    for axis, dim in sides:
        count = lax.axis_size(axis)
        ends = count - 1
        head = lax.slice_in_dim(cells, 0, width, axis=dim)
        tail = lax.slice_in_dim(cells, cells.shape[dim] - width, cells.shape[dim], axis=dim)
        cells = jnp.concatenate(
            [
                lax.ppermute(tail, axis, [(i, (i + 1) % count) for i in range(ends)]),
                cells,
                lax.ppermute(head, axis, [((i + 1) % count, i) for i in range(ends)]),
            ],
            axis=dim,
        )
    return cells


def layer_norm(values, gain):
    values = values.astype(jnp.float32)
    center = values - jnp.mean(values, axis=-1, keepdims=True)
    spread = jnp.mean(center * center, axis=-1, keepdims=True)
    return (center * lax.rsqrt(spread + EPS) * gain).astype(jnp.bfloat16)


def page_member(window_ids, page_windows):
    page_ends = jnp.cumsum(page_windows)
    page_starts = page_ends - page_windows
    return (window_ids[:, None] >= page_starts[None, :]) & (
        window_ids[:, None] < page_ends[None, :]
    )


def window_geometry(window_ids, page_windows, page_width):
    page_ends = jnp.cumsum(page_windows)
    page_starts = page_ends - page_windows
    member = page_member(window_ids, page_windows).astype(jnp.int32)
    begin = jnp.sum(member * page_starts[None, :], axis=1)
    across = jnp.sum(member * page_width[None, :], axis=1)
    total = jnp.sum(member * page_windows[None, :], axis=1)
    inside = window_ids - begin
    grid_row = inside // across
    grid_col = inside - grid_row * across
    rows_near = jnp.stack([grid_row + pair[0] for pair in OFFSETS], axis=1)
    cols_near = jnp.stack([grid_col + pair[1] for pair in OFFSETS], axis=1)
    place = rows_near * across[:, None] + cols_near
    valid = (
        (cols_near >= 0)
        & (cols_near < across[:, None])
        & (rows_near >= 0)
        & (place < total[:, None])
    )
    return (begin[:, None] + place, valid)


def edge_range(offset_value):
    if offset_value < 0:
        return (WIN - HALO, WIN)
    if offset_value > 0:
        return (0, HALO)
    return (0, WIN)


def gather_keys(grid_vals, tile_index, valid):
    count = tile_index.shape[0]
    feats = grid_vals.shape[-1]
    pieces = []
    keeps = []
    for number, pair in enumerate(OFFSETS):
        row_lo, row_hi = edge_range(pair[0])
        col_lo, col_hi = edge_range(pair[1])
        strip = grid_vals[:, row_lo:row_hi, col_lo:col_hi]
        picked = jnp.take(strip, tile_index[:, number], axis=0)
        picked = picked.reshape(count, -1, feats)
        pieces.append(picked)
        keeps.append(jnp.broadcast_to(valid[:, number : number + 1], (count, picked.shape[1])))
    return (jnp.concatenate(pieces, axis=1), jnp.concatenate(keeps, axis=1))


def attention(query, keys, values, mask, heads):
    count, qlen, width = query.shape
    depth = width // heads
    q_heads = query.reshape(count, qlen, heads, depth)
    k_heads = keys.reshape(count, -1, heads, depth)
    v_heads = values.reshape(count, -1, heads, depth)
    scores = jnp.einsum(
        "nqhd,nkhd->nhqk", q_heads, k_heads, preferred_element_type=jnp.float32
    ) / math.sqrt(depth)
    scores = jnp.where(mask[:, None], scores, -1e30)
    top_score = jnp.max(scores, axis=-1, keepdims=True)
    weights = jnp.exp(scores - top_score)
    probs = (weights / jnp.sum(weights, axis=-1, keepdims=True)).astype(jnp.bfloat16)
    output = jnp.einsum("nhqk,nkhd->nqhd", probs, v_heads, preferred_element_type=jnp.float32)
    return output.reshape(count, qlen, width).astype(jnp.bfloat16)


def shards(
    tokens,
    ln_gain,
    attn_weight,
    attn_proj,
    page_gain,
    page_weight,
    page_proj,
    page_windows,
    page_width,
    doc_pages,
):
    win_count = tokens.shape[0] // (WIN * WIN)
    local_width = attn_weight.shape[2]
    local_heads = local_width // HDIM
    feats = 2 * local_width
    normed = layer_norm(tokens, ln_gain)
    qkv = jnp.dot(
        normed, attn_weight.reshape(D, 3 * local_width), preferred_element_type=jnp.float32
    ).astype(jnp.bfloat16)
    queries = qkv[:, :local_width].reshape(win_count, WIN * WIN, local_width)
    keyvals = qkv[:, local_width:].reshape(win_count, WIN * WIN, feats)
    extended = with_halo(keyvals, (("pack", 0),), HALO_WIN)
    grid_vals = extended.reshape(extended.shape[0], WIN, WIN, feats)
    offset_start = lax.axis_index("pack") * win_count
    window_ids = offset_start + jnp.arange(win_count, dtype=jnp.int32)
    neighbor, valid = window_geometry(window_ids, page_windows, page_width)
    own_index = jnp.arange(win_count, dtype=jnp.int32)[:, None] + HALO_WIN
    tile_index = jnp.where(valid, neighbor - offset_start + HALO_WIN, own_index)

    def attend(block):
        query_block, index_block, valid_block = block
        region, keep = gather_keys(grid_vals, index_block, valid_block)
        return attention(
            query_block,
            region[..., :local_width],
            region[..., local_width:],
            keep[:, None, :],
            local_heads,
        )

    pairs = win_count // 2
    mixed = lax.map(
        attend,
        (
            queries.reshape(pairs, 2, WIN * WIN, local_width),
            tile_index.reshape(pairs, 2, 9),
            valid.reshape(pairs, 2, 9),
        ),
    )
    mixed = mixed.reshape(win_count * WIN * WIN, local_width)
    member = page_member(window_ids, page_windows).astype(jnp.float32)
    token_sums = jnp.sum(tokens.reshape(win_count, WIN * WIN, D), axis=1, dtype=jnp.float32)
    mixed_sums = jnp.sum(
        mixed.reshape(win_count, WIN * WIN, local_width), axis=1, dtype=jnp.float32
    )
    page_tokens = jnp.dot(member.T, token_sums, precision=lax.Precision.HIGHEST)
    page_mixed = jnp.dot(member.T, mixed_sums, precision=lax.Precision.HIGHEST)
    proj_local = attn_proj.astype(jnp.float32)
    counts = WIN * WIN * page_windows.astype(jnp.float32)
    total_tokens, total_mixed = (
        lax.psum(page_tokens.astype(jnp.bfloat16), "pack").astype(jnp.float32),
        lax.psum(page_mixed.astype(jnp.bfloat16), "pack").astype(jnp.float32),
    )
    projected = lax.psum(
        jnp.dot(total_mixed, proj_local, precision=lax.Precision.HIGHEST).astype(jnp.bfloat16),
        "head",
    ).astype(jnp.float32)
    pooled = (total_tokens + projected) / counts[:, None]
    page_count = page_windows.shape[0]
    page_normed = layer_norm(pooled, page_gain)
    page_qkv = jnp.dot(
        page_normed, page_weight.reshape(D, 3 * local_width), preferred_element_type=jnp.float32
    ).astype(jnp.bfloat16)
    doc_ends = jnp.cumsum(doc_pages)
    page_ids = jnp.arange(page_count, dtype=jnp.int32)
    doc_of = jnp.sum((page_ids[:, None] >= doc_ends[None, :]).astype(jnp.int32), axis=1)
    same_doc = doc_of[:, None] == doc_of[None, :]
    context = attention(
        page_qkv[None, :, :local_width],
        page_qkv[None, :, local_width : 2 * local_width],
        page_qkv[None, :, 2 * local_width :],
        same_doc[None],
        local_heads,
    )[0]
    branch = jnp.dot(context, page_proj, preferred_element_type=jnp.float32)
    my_share = lax.psum_scatter(
        branch.astype(jnp.bfloat16), "head", scatter_dimension=1, tiled=True
    ).astype(jnp.float32)
    column_start = lax.axis_index("head") * my_share.shape[1]
    page_out = lax.dynamic_slice_in_dim(pooled, column_start, my_share.shape[1], 1) + my_share
    return (mixed, page_out)


def solution(mesh):
    placed = (
        P(("rep", "pack"), None),
        P(),
        P(None, None, "head"),
        P("head", None),
        P(),
        P(None, None, "head"),
        P("head", None),
        P("rep"),
        P("rep"),
        P("rep"),
    )
    return jax.shard_map(
        shards,
        mesh=mesh,
        in_specs=placed,
        out_specs=(P(("rep", "pack"), "head"), P("rep", "head")),
        check_vma=False,
    )
```

profile of v0, /device:TPU:0, one launch (start us, length us, event | category | flops | bytes accessed | tf_op | source)
XLA Modules:
  0.0 700.1 jit_solution(7948608832417478910)
XLA Ops:
  18.7 13.9 %convolution_convert_fusion = bf16[3072,1536]{1,0:T(8,128)(2,1)S(1)} fusion(bf16[1024,1536]{0,1:T(8,128)(2,1)} %bitcast.90, bf16[3072,1024]{1,0:T(8,128)(2,1)} %param.18, f32[1024]{0:T(1024)S(1)} %copy-done.15, f32[3072]{0:T(1024)S(1)} %add_rsqrt_fusion, f32[3072]{0:T(1024)S(1)} %broadcast_multiply_fusion), kind=kOutput, calls=%fused_computation.83 | convolution fusion | flops 9684123648 | bytes 18903040 | tf_op jit(solution)/shard_map/dot_general | solution.py:131
  61.2 9.8 %pad_maximum_fusion = bf16[20,16,16,1024]{3,2,1,0:T(8,128)(2,1)} fusion(bf16[4,16,16,1024]{3,2,1,0:T(8,128)(2,1)} %bitcast.15, bf16[12,16,16,1024]{3,2,1,0:T(8,128)(2,1)} %bitcast.84, bf16[4,16,16,1024]{3,2,1,0:T(8,128)(2,1)S(1)} %bitcast.91), kind=kLoop, calls=%fused_computation.84 | loop fusion | flops 10485760 | bytes 20971520 | tf_op jit(solution)/shard_map/concatenate | solution.py:25
  71.0 494.4 %while.10 = (s32[]{:T(128)}, bf16[6,2,256,512]{2,3,1,0:T(8,128)(2,1)}, bf16[20,16,16,1024]{3,2,1,0:T(8,128)(2,1)}, s32[6,2,9]{2,1,0:T(2,128)S(1)}, pred[6,2,9]{2...) while((s32[]{:T(128)}, bf16[6,2,256,512]{2,3,1,0:T(8,128)(2,1)}, ...), condition=%wide.region_9.13_spmd, body=%wide.region_6.12_spmd.sunk | while | flops 633743104 | bytes 95790912 | solution.py:156
  84.5 9.3 %fusion.68 = (bf16[20,16,4,1024]{3,2,1,0:T(4,128)(2,1)}, bf16[20,16,4,1024]{3,2,1,0:T(4,128)(2,1)}) fusion(bf16[20,16,16,1024]{3,2,1,0:T(8,128)(2,1)} %get-tuple-element.283), kind=kLoop, calls=%fused_computation.141.clone.1 | loop fusion | bytes 10485760 | tf_op jit(solution)/shard_map/while/body/eval_jaxpr/slice | solution.py:89
  119.7 7.1 %concatenate.26 = bf16[2,576,1024]{1,2,0:T(8,128)(2,1)} concatenate(bf16[2,16,1024]{1,2,0:T(8,128)(2,1)} %copy.137, bf16[2,64,1024]{1,2,0:T(8,128)(2,1)} %copy.138, bf16[2,16,1024]{1,2,0:T(8,128)(2,1)} %copy.139, bf16[2,64,1024]{1,2,0:T(8,128)(2,1)} %copy.140, bf16[2,256,1024]{1,2,0:T(8,128)(2,1)S(1)} %broadcast_select_fusion.22, bf16[2,64,1024]{1,2,0:T(8,128)(2,1)} %copy.142, ...), dimensions={1} | concatenate | bytes 4718592 | tf_op jit(solution)/shard_map/while/body/eval_jaxpr/concatenate | solution.py:94
  132.3 12.3 %fusion.70 = (f32[2,16,256]{2,1,0:T(8,128)S(1)}, f32[2,16,256,576]{2,3,1,0:T(8,128)}) fusion(pred[2,576]{1,0:T(4,128)(4,1)S(1)} %concatenate.27, bf16[2,256,16,32]{1,3,2,0:T(8,128)(2,1)S(1)} %bitcast.85, bf16[2,576,16,32]{1,3,2,0:T(8,128)(2,1)} %bitcast.81), kind=kOutput, calls=%fused_computation.143.clone.1 | convolution fusion | flops 320864832 | bytes 20612224 | tf_op jit(solution)/shard_map/while/body/eval_jaxpr/sub | solution.py:108
  144.6 8.1 %fusion.71 = bf16[2,16,32,256]{3,2,1,0:T(8,128)(2,1)S(1)} fusion(bf16[2,576,16,32]{1,3,2,0:T(8,128)(2,1)S(1)} %bitcast.80, f32[2,16,256,576]{2,3,1,0:T(8,128)} %get-tuple-element.265, f32[2,16,256]{2,1,0:T(8,128)S(1)} %get-tuple-element.266), kind=kOutput, calls=%fused_computation.19.clone.1 | convolution fusion | flops 311689216 | bytes 20611072 | tf_op jit(solution)/shard_map/while/body/eval_jaxpr/nhqk,nkhd->nqhd/dot_general | solution.py:110
  167.0 9.3 %fusion.68 = (bf16[20,16,4,1024]{3,2,1,0:T(4,128)(2,1)}, bf16[20,16,4,1024]{3,2,1,0:T(4,128)(2,1)}) fusion(bf16[20,16,16,1024]{3,2,1,0:T(8,128)(2,1)} %get-tuple-element.283), kind=kLoop, calls=%fused_computation.141.clone.1 | loop fusion | bytes 10485760 | tf_op jit(solution)/shard_map/while/body/eval_jaxpr/slice | solution.py:89
  214.7 12.3 %fusion.70 = (f32[2,16,256]{2,1,0:T(8,128)S(1)}, f32[2,16,256,576]{2,3,1,0:T(8,128)}) fusion(pred[2,576]{1,0:T(4,128)(4,1)S(1)} %concatenate.27, bf16[2,256,16,32]{1,3,2,0:T(8,128)(2,1)S(1)} %bitcast.85, bf16[2,576,16,32]{1,3,2,0:T(8,128)(2,1)} %bitcast.81), kind=kOutput, calls=%fused_computation.143.clone.1 | convolution fusion | flops 320864832 | bytes 20612224 | tf_op jit(solution)/shard_map/while/body/eval_jaxpr/sub | solution.py:108
  227.0 8.1 %fusion.71 = bf16[2,16,32,256]{3,2,1,0:T(8,128)(2,1)S(1)} fusion(bf16[2,576,16,32]{1,3,2,0:T(8,128)(2,1)S(1)} %bitcast.80, f32[2,16,256,576]{2,3,1,0:T(8,128)} %get-tuple-element.265, f32[2,16,256]{2,1,0:T(8,128)S(1)} %get-tuple-element.266), kind=kOutput, calls=%fused_computation.19.clone.1 | convolution fusion | flops 311689216 | bytes 20611072 | tf_op jit(solution)/shard_map/while/body/eval_jaxpr/nhqk,nkhd->nqhd/dot_general | solution.py:110
  249.4 9.3 %fusion.68 = (bf16[20,16,4,1024]{3,2,1,0:T(4,128)(2,1)}, bf16[20,16,4,1024]{3,2,1,0:T(4,128)(2,1)}) fusion(bf16[20,16,16,1024]{3,2,1,0:T(8,128)(2,1)} %get-tuple-element.283), kind=kLoop, calls=%fused_computation.141.clone.1 | loop fusion | bytes 10485760 | tf_op jit(solution)/shard_map/while/body/eval_jaxpr/slice | solution.py:89
  297.1 12.3 %fusion.70 = (f32[2,16,256]{2,1,0:T(8,128)S(1)}, f32[2,16,256,576]{2,3,1,0:T(8,128)}) fusion(pred[2,576]{1,0:T(4,128)(4,1)S(1)} %concatenate.27, bf16[2,256,16,32]{1,3,2,0:T(8,128)(2,1)S(1)} %bitcast.85, bf16[2,576,16,32]{1,3,2,0:T(8,128)(2,1)} %bitcast.81), kind=kOutput, calls=%fused_computation.143.clone.1 | convolution fusion | flops 320864832 | bytes 20612224 | tf_op jit(solution)/shard_map/while/body/eval_jaxpr/sub | solution.py:108
  309.4 8.1 %fusion.71 = bf16[2,16,32,256]{3,2,1,0:T(8,128)(2,1)S(1)} fusion(bf16[2,576,16,32]{1,3,2,0:T(8,128)(2,1)S(1)} %bitcast.80, f32[2,16,256,576]{2,3,1,0:T(8,128)} %get-tuple-element.265, f32[2,16,256]{2,1,0:T(8,128)S(1)} %get-tuple-element.266), kind=kOutput, calls=%fused_computation.19.clone.1 | convolution fusion | flops 311689216 | bytes 20611072 | tf_op jit(solution)/shard_map/while/body/eval_jaxpr/nhqk,nkhd->nqhd/dot_general | solution.py:110
  331.7 9.3 %fusion.68 = (bf16[20,16,4,1024]{3,2,1,0:T(4,128)(2,1)}, bf16[20,16,4,1024]{3,2,1,0:T(4,128)(2,1)}) fusion(bf16[20,16,16,1024]{3,2,1,0:T(8,128)(2,1)} %get-tuple-element.283), kind=kLoop, calls=%fused_computation.141.clone.1 | loop fusion | bytes 10485760 | tf_op jit(solution)/shard_map/while/body/eval_jaxpr/slice | solution.py:89
  379.4 12.3 %fusion.70 = (f32[2,16,256]{2,1,0:T(8,128)S(1)}, f32[2,16,256,576]{2,3,1,0:T(8,128)}) fusion(pred[2,576]{1,0:T(4,128)(4,1)S(1)} %concatenate.27, bf16[2,256,16,32]{1,3,2,0:T(8,128)(2,1)S(1)} %bitcast.85, bf16[2,576,16,32]{1,3,2,0:T(8,128)(2,1)} %bitcast.81), kind=kOutput, calls=%fused_computation.143.clone.1 | convolution fusion | flops 320864832 | bytes 20612224 | tf_op jit(solution)/shard_map/while/body/eval_jaxpr/sub | solution.py:108
  391.7 8.1 %fusion.71 = bf16[2,16,32,256]{3,2,1,0:T(8,128)(2,1)S(1)} fusion(bf16[2,576,16,32]{1,3,2,0:T(8,128)(2,1)S(1)} %bitcast.80, f32[2,16,256,576]{2,3,1,0:T(8,128)} %get-tuple-element.265, f32[2,16,256]{2,1,0:T(8,128)S(1)} %get-tuple-element.266), kind=kOutput, calls=%fused_computation.19.clone.1 | convolution fusion | flops 311689216 | bytes 20611072 | tf_op jit(solution)/shard_map/while/body/eval_jaxpr/nhqk,nkhd->nqhd/dot_general | solution.py:110
  414.1 9.3 %fusion.68 = (bf16[20,16,4,1024]{3,2,1,0:T(4,128)(2,1)}, bf16[20,16,4,1024]{3,2,1,0:T(4,128)(2,1)}) fusion(bf16[20,16,16,1024]{3,2,1,0:T(8,128)(2,1)} %get-tuple-element.283), kind=kLoop, calls=%fused_computation.141.clone.1 | loop fusion | bytes 10485760 | tf_op jit(solution)/shard_map/while/body/eval_jaxpr/slice | solution.py:89
  461.8 12.3 %fusion.70 = (f32[2,16,256]{2,1,0:T(8,128)S(1)}, f32[2,16,256,576]{2,3,1,0:T(8,128)}) fusion(pred[2,576]{1,0:T(4,128)(4,1)S(1)} %concatenate.27, bf16[2,256,16,32]{1,3,2,0:T(8,128)(2,1)S(1)} %bitcast.85, bf16[2,576,16,32]{1,3,2,0:T(8,128)(2,1)} %bitcast.81), kind=kOutput, calls=%fused_computation.143.clone.1 | convolution fusion | flops 320864832 | bytes 20612224 | tf_op jit(solution)/shard_map/while/body/eval_jaxpr/sub | solution.py:108
  474.1 8.1 %fusion.71 = bf16[2,16,32,256]{3,2,1,0:T(8,128)(2,1)S(1)} fusion(bf16[2,576,16,32]{1,3,2,0:T(8,128)(2,1)S(1)} %bitcast.80, f32[2,16,256,576]{2,3,1,0:T(8,128)} %get-tuple-element.265, f32[2,16,256]{2,1,0:T(8,128)S(1)} %get-tuple-element.266), kind=kOutput, calls=%fused_computation.19.clone.1 | convolution fusion | flops 311689216 | bytes 20611072 | tf_op jit(solution)/shard_map/while/body/eval_jaxpr/nhqk,nkhd->nqhd/dot_general | solution.py:110
  496.4 9.3 %fusion.68 = (bf16[20,16,4,1024]{3,2,1,0:T(4,128)(2,1)}, bf16[20,16,4,1024]{3,2,1,0:T(4,128)(2,1)}) fusion(bf16[20,16,16,1024]{3,2,1,0:T(8,128)(2,1)} %get-tuple-element.283), kind=kLoop, calls=%fused_computation.141.clone.1 | loop fusion | bytes 10485760 | tf_op jit(solution)/shard_map/while/body/eval_jaxpr/slice | solution.py:89
  544.1 12.3 %fusion.70 = (f32[2,16,256]{2,1,0:T(8,128)S(1)}, f32[2,16,256,576]{2,3,1,0:T(8,128)}) fusion(pred[2,576]{1,0:T(4,128)(4,1)S(1)} %concatenate.27, bf16[2,256,16,32]{1,3,2,0:T(8,128)(2,1)S(1)} %bitcast.85, bf16[2,576,16,32]{1,3,2,0:T(8,128)(2,1)} %bitcast.81), kind=kOutput, calls=%fused_computation.143.clone.1 | convolution fusion | flops 320864832 | bytes 20612224 | tf_op jit(solution)/shard_map/while/body/eval_jaxpr/sub | solution.py:108
  556.5 8.1 %fusion.71 = bf16[2,16,32,256]{3,2,1,0:T(8,128)(2,1)S(1)} fusion(bf16[2,576,16,32]{1,3,2,0:T(8,128)(2,1)S(1)} %bitcast.80, f32[2,16,256,576]{2,3,1,0:T(8,128)} %get-tuple-element.265, f32[2,16,256]{2,1,0:T(8,128)S(1)} %get-tuple-element.266), kind=kOutput, calls=%fused_computation.19.clone.1 | convolution fusion | flops 311689216 | bytes 20611072 | tf_op jit(solution)/shard_map/while/body/eval_jaxpr/nhqk,nkhd->nqhd/dot_general | solution.py:110
  568.6 87.3 %psum.22 = bf16[48,512]{1,0:T(8,128)(2,1)S(1)} all-reduce(bf16[48,512]{1,0:T(8,128)(2,1)S(1)} %convolution_convert_fusion.6), channel_id=1, replica_groups=mesh['pack'=16,'head'=2,'rep'=1] {'pack'}, use_global_device_ids=true, to_apply=%region_13.17 | all-reduce | flops 24576 | bytes 98304 | tf_op jit(solution)/shard_map/psum | solution.py:176
  661.5 13.8 %all-reduce.5.cloned.1.call-done = bf16[48,1024]{1,0:T(8,128)(2,1)} async-done(((bf16[48,1024]{1,0:T(8,128)(2,1)}), bf16[48,1024]{1,0:T(8,128)(2,1)}) %all-reduce.5.cloned.1.call-update) | async-done | bytes 98320 | tf_op jit(solution)/shard_map/psum | solution.py:178
  (535 shorter events, 375.1 us)
Async XLA Ops:
  7.2 648.7 %copy-start = (bf16[512,1024]{1,0:T(8,128)(2,1)S(1)}, bf16[512,1024]{1,0:T(8,128)(2,1)}, u32[]{:S(2)}) copy-start(bf16[512,1024]{1,0:T(8,128)(2,1)} %param.21) | copy-start | bytes 3145732
  7.2 654.3 %all-reduce.3.cloned.1.call-start = ((), (), s32[]{:S(2)}) async-start(), calls=%async_computation.1 | async-start | bytes 196608 | tf_op jit(solution)/shard_map/psum | solution.py:175
  7.2 4.7 copy-start.1
  14.0 4.7 copy-start.15
  32.6 3.6 copy-start.2
  36.2 6.3 copy-start.12
  38.7 22.5 %collective-permute-start = (bf16[4,256,1024]{2,1,0:T(8,128)(2,1)}, bf16[4,256,1024]{2,1,0:T(8,128)(2,1)S(1)}, u32[]{:S(2)}, u32[]{:S(2)}) collective-permute-start(bf16[4,256,1024]{2,1,0:T(8,128)(2,1)} %bitcast.11), channel_id=1, source_target_pairs={{0,2},{2,4},{4,6},{6,8},{8,10},{10,12},{12,14},{14,16},{16,18},{18... | collective-permute-start | bytes 6291464 | tf_op jit(solution)/shard_map/ppermute | solution.py:27
  41.2 20.0 %collective-permute-start.1 = (bf16[4,256,1024]{2,1,0:T(8,128)(2,1)}, bf16[4,256,1024]{2,1,0:T(8,128)(2,1)}, u32[]{:S(2)}, u32[]{:S(2)}) collective-permute-start(bf16[4,256,1024]{2,1,0:T(8,128)(2,1)} %bitcast.14), channel_id=1, source_target_pairs={{2,0},{4,2},{6,4},{8,6},{10,8},{12,10},{14,12},{16,14},{18,16},{20... | collective-permute-start | bytes 6291464 | tf_op jit(solution)/shard_map/ppermute | solution.py:29
  42.8 5.6 copy-start.5
  42.8 5.5 copy-start.7
  42.9 5.5 copy-start.14
  47.1 8.0 %copy-start.9 = (s32[12]{0:T(128)}, s32[12]{0:T(128)S(1)}, u32[]{:S(2)}) copy-start(s32[12]{0:T(128)S(1)} %iota_add_fusion) | copy-start | bytes 148
  48.2 627.1 %all-reduce.5.cloned.1.call-start = ((), (), s32[]{:S(2)}) async-start(), calls=%async_computation.2 | async-start | bytes 196608 | tf_op jit(solution)/shard_map/psum | solution.py:178
  55.1 4.7 copy-start.16
  565.4 2.8 copy-start.6
  565.4 2.9 copy-start.8
  565.4 2.9 copy-start.10
  565.4 91.5 %copy-start.13 = (s32[48]{0:T(128)S(1)}, s32[48]{0:T(128)}, u32[]{:S(2)}) copy-start(s32[48]{0:T(128)} %param.25) | copy-start | bytes 580
  656.8 35.3 %reduce-scatter.2.cloned.1.call-start = ((), (), s32[]{:S(2)}) async-start(), calls=%async_computation.3 | async-start | bytes 147456 | tf_op jit(solution)/shard_map/reduce_scatter | solution.py:200
  656.9 19.8 %copy-start.11 = (f32[1024]{0:T(1024)S(1)}, f32[1024]{0:T(1024)}, u32[]{:S(2)}) copy-start(f32[1024]{0:T(1024)} %param.22) | copy-start | bytes 12292
  661.5 18.5 %copy-start.4 = (pred[48,48]{0,1:T(8,128)(4,1)S(1)}, pred[48,48]{0,1:T(8,128)(4,1)}, u32[]{:S(2)}) copy-start(pred[48,48]{0,1:T(8,128)(4,1)} %broadcast_compare_fusion) | copy-start | bytes 6916
  676.6 4.3 copy-start.3
Sparse Core Ops, SparseCore 0:
  48.3 101.5 all-reduce.2
  656.9 18.3 all-reduce.4
  682.1 9.9 reduce-scatter.1
where the time goes:
time: 705 us; the launch traced here: 700 us
  local copies, waits for them, and re-layouts  393 us (56%)
  matrix products  143 us (20%)
  blocking collectives  87.3 us (12%)
  other arithmetic  37.5 us (5%)
  waiting for transfers between devices  19.3 us (3%)
  between operations  14.1 us (2%)
    slice x18, local copies, waits for them, and re-layouts, gather_keys(): strip = grid_vals[:, row_lo:row_hi, col_lo:col_hi]  120 us
    gather x60, local copies, waits for them, and re-layouts, gather_keys(): picked = jnp.take(strip, tile_index[:, number], axis=0)  110 us
    psum x1, blocking collectives, shards(): lax.psum(page_mixed.astype(jnp.bfloat16), 'pack').astype(jnp.float32)  87.3 us
    sub x7, matrix products, attention(): weights = jnp.exp(scores - top_score)  74.1 us
    reshape x84, local copies, waits for them, and re-layouts, gather_keys(): picked = picked.reshape(count, -1, feats)  50.1 us
    dot_general x7, matrix products, attention(): jnp.einsum('nhqk,nkhd->nqhd', probs, v_heads, preferred_element_type=jnp....  48.6 us
    concatenate x12, local copies, waits for them, and re-layouts, gather_keys(): return (jnp.concatenate(pieces, axis=1), jnp.concatenate(keeps, axis=1))  43.5 us
    slice x6, local copies, waits for them, and re-layouts, attend(): region[..., :local_width]  18 us
  transfers between devices with their start and end apart: 5, of which 2 were waited for; matrix products, arithmetic and copies ran while one was open for 76% of the time, Pallas kernels for 0%

commit v1 on v0

v1 whole, which is shorter than its diff:
```python
import math

import jax
import jax.numpy as jnp
import numpy as np
from jax import lax
from jax.experimental import pallas as pl
from jax.experimental.pallas import tpu as pltpu
from jax.sharding import PartitionSpec as P

D = 1024
HDIM = 32
WIN = 16
HALO = 4
HALO_WIN = 4
TOK = WIN * WIN
STRIP = WIN * HALO
CORNER = HALO * HALO
SIDE_KEYS = 4 * STRIP + 4 * CORNER
KEYS = TOK + SIDE_KEYS
SIDE_LANES = 384
EPS = 1e-05
LOG2E = 1.4426950408889634
OFFSETS = ((-1, 0), (1, 0), (0, -1), (0, 1), (-1, -1), (-1, 1), (1, -1), (1, 1))


def near(offset_value):
    if offset_value < 0:
        return range(WIN - HALO, WIN)
    if offset_value > 0:
        return range(0, HALO)
    return range(0, WIN)


def strip_tokens():
    return [[r * WIN + c for r in near(a) for c in near(b)] for a, b in OFFSETS]


def one_hot(rows, width):
    table = np.zeros((SIDE_KEYS, width), np.float32)
    for i, j in enumerate(rows):
        if j >= 0:
            table[i, j] = 1.0
    padded = np.zeros((width, SIDE_LANES), np.float32)
    padded[:, :SIDE_KEYS] = table.T
    return jnp.asarray(table, jnp.bfloat16), jnp.asarray(padded, jnp.bfloat16)


def selections():
    strips = strip_tokens()
    flat = [t for s in strips for t in s]
    own = one_hot(flat, TOK)
    out = [own]
    for row_piece, col_piece in ((0, 2), (1, 3)):
        where = {t: i for i, t in enumerate(strips[row_piece])}
        cols = {t: STRIP + i for i, t in enumerate(strips[col_piece])}
        rows = []
        for number, strip in enumerate(strips):
            same = OFFSETS[number][0] == OFFSETS[row_piece][0]
            for t in strip:
                if same:
                    rows.append(where[t])
                elif number == col_piece:
                    rows.append(cols[t])
                else:
                    rows.append(-1)
        out.append(one_hot(rows, 2 * STRIP))
    return out


def nt_dot(a, b):
    return lax.dot_general(a, b, (((1,), (1,)), ((), ())), preferred_element_type=jnp.float32)


def nn_dot(a, b):
    return jnp.dot(a, b, preferred_element_type=jnp.float32)


def normalize(values, gain):
    center = values - jnp.mean(values, axis=-1, keepdims=True)
    spread = jnp.mean(center * center, axis=-1, keepdims=True)
    return (center * lax.rsqrt(spread + EPS) * gain).astype(jnp.bfloat16)


def window_kernel(
    win_count,
    width,
    slot_ref,
    bias_ref,
    tok_ref,
    halo_ref,
    gain_ref,
    wq_ref,
    wk_ref,
    wv_ref,
    sel_ref,
    selt_ref,
    selp_ref,
    selpt_ref,
    seln_ref,
    selnt_ref,
    mixed_ref,
    tsum_ref,
    msum_ref,
    qt_s,
    ko_s,
    ks_s,
    vo_s,
    vs_s,
    ke_s,
    ve_s,
    qz_s,
    ot_s,
):
    step = pl.program_id(0)
    groups = width // 128
    per = 128 // HDIM

    def put_side(slot, k, vt, sel, selt):
        ks = nn_dot(sel, k).astype(jnp.bfloat16)
        for g in range(groups):
            ks_s[slot, g] = ks[:, g * 128 : (g + 1) * 128]
        vs_s[slot] = nn_dot(vt, selt).astype(jnp.bfloat16)

    @pl.when(step == 0)
    def _():
        qz_s[...] = jnp.zeros_like(qz_s)
        gain = gain_ref[...]
        normed = normalize(halo_ref[...].astype(jnp.float32), gain)
        half = (HALO_WIN + 1) * STRIP
        for side, sel, selt, first in (
            (0, selp_ref, selpt_ref, 0),
            (1, seln_ref, selnt_ref, HALO_WIN + win_count),
        ):
            base = side * half
            for i in range(HALO_WIN):
                piece = jnp.concatenate(
                    [
                        normed[base + i * STRIP : base + (i + 1) * STRIP],
                        normed[base + HALO_WIN * STRIP : base + half],
                    ],
                    axis=0,
                )
                k = nn_dot(piece, wk_ref[...]).astype(jnp.bfloat16)
                vt = nt_dot(wv_ref[...], piece).astype(jnp.bfloat16)
                put_side(first + i, k, vt, sel[...], selt[...])

    @pl.when(step < win_count)
    def _():
        values = tok_ref[...].astype(jnp.float32)
        tsum_ref[0] = jnp.sum(values, axis=0, keepdims=True)
        normed = normalize(values, gain_ref[...])
        qt_s[step] = nt_dot(wq_ref[...], normed).astype(jnp.bfloat16)
        k = nn_dot(normed, wk_ref[...]).astype(jnp.bfloat16)
        for g in range(groups):
            ko_s[step, g] = k[:, g * 128 : (g + 1) * 128]
        vt = nt_dot(wv_ref[...], normed).astype(jnp.bfloat16)
        vo_s[step] = vt
        put_side(step + HALO_WIN, k, vt, sel_ref[...], selt_ref[...])

    @pl.when(step >= win_count)
    def _():
        win = step - win_count
        slots = [slot_ref[win * 8 + i] for i in range(8)]
        biases = [bias_ref[win * 8 + i] for i in range(8)]
        ke_s[:, :TOK] = ko_s[win]
        ve_s[:, :TOK] = vo_s[win]
        place = 0
        for i in range(8):
            size = STRIP if i < 4 else CORNER
            ke_s[:, TOK + place : TOK + place + size] = ks_s[slots[i], :, place : place + size]
            place += size
        lane = lax.broadcasted_iota(jnp.int32, (width, 128), 1)
        for pair in range(2):
            lo = pair * 128
            ve_s[:, TOK + lo : TOK + lo + 128] = jnp.where(
                lane < STRIP,
                vs_s[slots[2 * pair], :, lo : lo + 128],
                vs_s[slots[2 * pair + 1], :, lo : lo + 128],
            )
        corner = [vs_s[slots[4 + i], :, 256:384] for i in range(4)]
        ve_s[:, TOK + 256 : TOK + 384] = jnp.where(
            lane < 2 * CORNER,
            jnp.where(lane < CORNER, corner[0], corner[1]),
            jnp.where(lane < 3 * CORNER, corner[2], corner[3]),
        )
        for h in range(width // HDIM):
            lo = (h % per) * HDIM
            qz_s[h, lo : lo + HDIM] = qt_s[win, h * HDIM : (h + 1) * HDIM]

        factor = LOG2E / math.sqrt(HDIM)

        def group(g, carry):
            for j in range(per):
                head = g * per + j
                scores = nn_dot(ke_s[g], qz_s[head])
                parts = [scores[:TOK] * factor]
                place = TOK
                for i in range(8):
                    size = STRIP if i < 4 else CORNER
                    parts.append(scores[place : place + size] * factor + biases[i])
                    place += size
                scaled = jnp.concatenate(parts, axis=0)
                top = jnp.max(scaled, axis=0, keepdims=True)
                weights = jnp.exp2(scaled - top)
                inverse = 1.0 / jnp.sum(weights, axis=0, keepdims=True)
                probs = (weights * inverse).astype(jnp.bfloat16)
                row = pl.multiple_of(head * HDIM, HDIM)
                ot_s[pl.ds(row, HDIM), :] = nn_dot(ve_s[pl.ds(row, HDIM), :KEYS], probs)
            return carry

        lax.fori_loop(0, groups, group, 0)
        mixed = ot_s[...].T.astype(jnp.bfloat16)
        mixed_ref[...] = mixed
        msum_ref[0] = jnp.sum(mixed.astype(jnp.float32), axis=0, keepdims=True)


def window_layer(tokens, halo, gain, weight, slots, biases):
    win_count = tokens.shape[0] // TOK
    width = weight.shape[2]
    groups = width // 128
    wq, wk, wv = weight[:, 0].T, weight[:, 1], weight[:, 2].T
    tables = [t for pair in selections() for t in pair]

    def whole(array):
        return pl.BlockSpec(
            array.shape, lambda i, *_: (0,) * array.ndim, pipeline_mode=pl.Buffered(1)
        )

    def first(i, *_):
        return jnp.minimum(i, win_count - 1)

    def second(i, *_):
        return jnp.maximum(i - win_count, 0)

    fixed = [halo, gain.reshape(1, D), wq, wk, wv] + tables
    slots_n = win_count + 2 * HALO_WIN
    bf = jnp.bfloat16
    return pl.pallas_call(
        lambda *refs: window_kernel(win_count, width, *refs),
        out_shape=(
            jax.ShapeDtypeStruct((win_count * TOK, width), bf),
            jax.ShapeDtypeStruct((win_count, 1, D), jnp.float32),
            jax.ShapeDtypeStruct((win_count, 1, width), jnp.float32),
        ),
        grid_spec=pltpu.PrefetchScalarGridSpec(
            num_scalar_prefetch=2,
            grid=(2 * win_count,),
            in_specs=[pl.BlockSpec((TOK, D), lambda i, *_: (first(i), 0))]
            + [whole(a) for a in fixed],
            out_specs=(
                pl.BlockSpec((TOK, width), lambda i, *_: (second(i), 0)),
                pl.BlockSpec((1, 1, D), lambda i, *_: (first(i), 0, 0)),
                pl.BlockSpec((1, 1, width), lambda i, *_: (second(i), 0, 0)),
            ),
            scratch_shapes=[
                pltpu.VMEM((win_count, width, TOK), bf),
                pltpu.VMEM((win_count, groups, TOK, 128), bf),
                pltpu.VMEM((slots_n, groups, SIDE_KEYS, 128), bf),
                pltpu.VMEM((win_count, width, TOK), bf),
                pltpu.VMEM((slots_n, width, SIDE_LANES), bf),
                pltpu.VMEM((groups, KEYS, 128), bf),
                pltpu.VMEM((width, TOK + SIDE_LANES), bf),
                pltpu.VMEM((width // HDIM, 128, TOK), bf),
                pltpu.VMEM((width, TOK), jnp.float32),
            ],
        ),
        compiler_params=pltpu.CompilerParams(vmem_limit_bytes=58 << 20),
        cost_estimate=pl.CostEstimate(
            flops=2 * win_count * TOK * (3 * D * width + 2 * KEYS * width),
            bytes_accessed=win_count * TOK * (2 * D + 2 * width),
            transcendentals=win_count * TOK * KEYS * width // HDIM,
        ),
    )(slots.reshape(-1), biases.reshape(-1), tokens, *fixed)


def halo_tokens(tokens):
    grid = tokens.reshape(-1, WIN, WIN, D)
    count = lax.axis_size("pack")
    tail = jnp.concatenate(
        [
            grid[-HALO_WIN:, WIN - HALO :].reshape(-1, D),
            grid[-1, :, WIN - HALO :].reshape(-1, D),
        ]
    )
    head = jnp.concatenate(
        [grid[:HALO_WIN, :HALO].reshape(-1, D), grid[0, :, :HALO].reshape(-1, D)]
    )
    before = lax.ppermute(tail, "pack", [(i, i + 1) for i in range(count - 1)])
    after = lax.ppermute(head, "pack", [(i + 1, i) for i in range(count - 1)])
    return jnp.concatenate([before, after])


def layer_norm(values, gain):
    values = values.astype(jnp.float32)
    return normalize(values, gain)


def page_member(window_ids, page_windows):
    page_ends = jnp.cumsum(page_windows)
    page_starts = page_ends - page_windows
    return (window_ids[:, None] >= page_starts[None, :]) & (
        window_ids[:, None] < page_ends[None, :]
    )


def window_geometry(window_ids, page_windows, page_width):
    page_ends = jnp.cumsum(page_windows)
    page_starts = page_ends - page_windows
    member = page_member(window_ids, page_windows).astype(jnp.int32)
    begin = jnp.sum(member * page_starts[None, :], axis=1)
    across = jnp.sum(member * page_width[None, :], axis=1)
    total = jnp.sum(member * page_windows[None, :], axis=1)
    inside = window_ids - begin
    grid_row = inside // across
    grid_col = inside - grid_row * across
    rows_near = jnp.stack([grid_row + pair[0] for pair in OFFSETS], axis=1)
    cols_near = jnp.stack([grid_col + pair[1] for pair in OFFSETS], axis=1)
    place = rows_near * across[:, None] + cols_near
    valid = (
        (cols_near >= 0)
        & (cols_near < across[:, None])
        & (rows_near >= 0)
        & (place < total[:, None])
    )
    return (begin[:, None] + place, valid)


def attention(query, keys, values, mask, heads):
    qlen, width = query.shape
    depth = width // heads
    q_heads = query.reshape(qlen, heads, depth)
    k_heads = keys.reshape(-1, heads, depth)
    v_heads = values.reshape(-1, heads, depth)
    scores = jnp.einsum(
        "qhd,khd->hqk", q_heads, k_heads, preferred_element_type=jnp.float32
    ) / math.sqrt(depth)
    scores = jnp.where(mask[None], scores, -1e30)
    top_score = jnp.max(scores, axis=-1, keepdims=True)
    weights = jnp.exp(scores - top_score)
    probs = (weights / jnp.sum(weights, axis=-1, keepdims=True)).astype(jnp.bfloat16)
    output = jnp.einsum("hqk,khd->qhd", probs, v_heads, preferred_element_type=jnp.float32)
    return output.reshape(qlen, width).astype(jnp.bfloat16)


def shards(
    tokens,
    ln_gain,
    attn_weight,
    attn_proj,
    page_gain,
    page_weight,
    page_proj,
    page_windows,
    page_width,
    doc_pages,
):
    win_count = tokens.shape[0] // TOK
    local_width = attn_weight.shape[2]
    local_heads = local_width // HDIM
    offset_start = lax.axis_index("pack") * win_count
    window_ids = offset_start + jnp.arange(win_count, dtype=jnp.int32)
    neighbor, valid = window_geometry(window_ids, page_windows, page_width)
    own_index = jnp.arange(win_count, dtype=jnp.int32)[:, None] + HALO_WIN
    slots = jnp.where(valid, neighbor - offset_start + HALO_WIN, own_index)
    biases = jnp.where(valid, 0.0, -1e30).astype(jnp.float32)
    halo = halo_tokens(tokens)
    mixed, token_sums, mixed_sums = window_layer(
        tokens, halo, ln_gain, attn_weight, slots, biases
    )
    member = page_member(window_ids, page_windows).astype(jnp.float32)
    highest = lax.Precision.HIGHEST
    page_tokens = jnp.dot(member.T, token_sums[:, 0], precision=highest)
    page_mixed = jnp.dot(member.T, mixed_sums[:, 0], precision=highest)
    projected = jnp.dot(page_mixed, attn_proj.astype(jnp.float32), precision=highest)
    share = jnp.where(lax.axis_index("head") == 0, 1.0, 0.0)
    counts = TOK * page_windows.astype(jnp.float32)
    total = lax.psum(page_tokens * share + projected, ("pack", "head"))
    pooled = total / counts[:, None]
    page_count = page_windows.shape[0]
    page_normed = layer_norm(pooled, page_gain)
    page_qkv = jnp.dot(
        page_normed, page_weight.reshape(D, 3 * local_width), preferred_element_type=jnp.float32
    ).astype(jnp.bfloat16)
    doc_ends = jnp.cumsum(doc_pages)
    page_ids = jnp.arange(page_count, dtype=jnp.int32)
    doc_of = jnp.sum((page_ids[:, None] >= doc_ends[None, :]).astype(jnp.int32), axis=1)
    same_doc = doc_of[:, None] == doc_of[None, :]
    context = attention(
        page_qkv[:, :local_width],
        page_qkv[:, local_width : 2 * local_width],
        page_qkv[:, 2 * local_width :],
        same_doc,
        local_heads,
    )
    branch = jnp.dot(context, page_proj, preferred_element_type=jnp.float32)
    my_share = lax.psum_scatter(
        branch.astype(jnp.bfloat16), "head", scatter_dimension=1, tiled=True
    ).astype(jnp.float32)
    column_start = lax.axis_index("head") * my_share.shape[1]
    page_out = lax.dynamic_slice_in_dim(pooled, column_start, my_share.shape[1], 1) + my_share
    return (mixed, page_out)


def solution(mesh):
    placed = (
        P(("rep", "pack"), None),
        P(),
        P(None, None, "head"),
        P("head", None),
        P(),
        P(None, None, "head"),
        P("head", None),
        P("rep"),
        P("rep"),
        P("rep"),
    )
    return jax.shard_map(
        shards,
        mesh=mesh,
        in_specs=placed,
        out_specs=(P(("rep", "pack"), "head"), P("rep", "head")),
        check_vma=False,
    )
```

time: 705 us -> 328 us (0.47)
  local copies, waits for them, and re-layouts: 393 us -> 14.5 us
  Pallas kernels: 0 us -> 141 us
  matrix products: 143 us -> 8.28 us
  waiting for transfers between devices: 19.3 us -> 136 us
  blocking collectives: 87.3 us -> 0 us
  other arithmetic: 37.5 us -> 9.01 us
    slice x34 -> x4, local copies, waits for them, and re-layouts: 153 us -> 5.62 us  [the longest x1 3.12 us: window_layer(): wq, wk, wv = (weight[:, 0].T, weight[:, 1], weight[:, 2].T)]
    pallas_call x0 -> x1, Pallas kernels: none -> 141 us  [window_layer(): pl.pallas_call(lambda *refs: window_kernel(win_count, width, *refs), out_...]
    psum x2 -> x1, waiting for transfers between devices: 13.8 us -> 125 us  [shards(): total = lax.psum(page_tokens * share + projected, ('pack', 'head'))]
    gather x60 -> x0, local copies, waits for them, and re-layouts: 110 us -> none  [gather_keys(): picked = jnp.take(strip, tile_index[:, number], axis=0)]
    psum x1 -> x0, blocking collectives: 87.3 us -> none  [shards(): lax.psum(page_mixed.astype(jnp.bfloat16), 'pack').astype(jnp.float32)]
    sub x7 -> x1, matrix products: 74.1 us -> 0.35 us  [attention(): weights = jnp.exp(scores - top_score)]
    dot_general x12 -> x5, matrix products: 65 us -> 4 us  [the longest x1 1.83 us: shards(): page_tokens = jnp.dot(member.T, token_sums[:, 0], precision=highest)]
    reshape x84 -> x3, local copies, waits for them, and re-layouts: 50.1 us -> 0.36 us  [the longest x1 0.12 us: attention(): k_heads = keys.reshape(-1, heads, depth)]
  transfers between devices with their start and end apart: 5 -> 4, of which waited for: 2 -> 2; matrix products, arithmetic and copies ran while one was open for 76% -> 4% of each run, Pallas kernels for 0% -> 0%
where the time goes in v1:
time: 328 us
  Pallas kernels  141 us (43%)
  waiting for transfers between devices  136 us (41%)
  local copies, waits for them, and re-layouts  14.5 us (4%)
  between operations  14.3 us (4%)
  other arithmetic  9.01 us (3%)
  matrix products  8.28 us (3%)
  starting transfers between devices  4.57 us (1%)
    pallas_call x1, Pallas kernels, window_layer(): pl.pallas_call(lambda *refs: window_kernel(win_count, width, *refs), out_...  141 us
    psum x1, waiting for transfers between devices, shards(): total = lax.psum(page_tokens * share + projected, ('pack', 'head'))  125 us
    reduce_scatter x1, waiting for transfers between devices, shards(): lax.psum_scatter(branch.astype(jnp.bfloat16), 'head', scatter_dimension=1...  11 us
    unnamed x15, local copies, waits for them, and re-layouts  7.36 us
  transfers between devices with their start and end apart: 4, of which 2 were waited for; matrix products, arithmetic and copies ran while one was open for 4% of the time, Pallas kernels for 0%

profile of v1, /device:TPU:0, one launch (start us, length us, event | category | flops | bytes accessed | tf_op | source)
XLA Modules:
  0.0 327.8 jit_solution(6267641061772847994)
XLA Ops:
  7.2 1.4 fusion.19
  8.6 1.1 fusion.20
  9.8 0.9 pad_maximum_fusion.1
  10.7 3.2 collective-permute-start
  13.9 0.9 pad_maximum_fusion.2
  14.8 1.3 collective-permute-start.1
  17.8 3.1 fusion.21
  21.0 1.3 copy.54
  22.3 1.3 copy.53
  23.9 0.6 broadcast_select_fusion
  24.5 0.5 add_select_fusion.refs_0_
  25.1 2.4 pad_maximum_fusion.refs_3_
  27.5 140.7 %shard_map.167 = (bf16[3072,512]{1,0:T(8,128)(2,1)}, f32[12,1,1024]{2,1,0:T(1,128)}, f32[12,1,512]{2,1,0:T(1,128)}) custom-call(s32[96]{0:T(128)} %add_select_fusion.refs_0_, f32[96]{0:T(128)} %get-tuple-element.13.refs_1_, bf16[3072,1024]{1,0:T(8,128)(2,1)} %refs_2_.1, bf16[640,1024]{1,0:T(8,128)(2,1)} %pad_maximum_fusion.refs_3_, f32[1,1024]{1,0:T(1,128)} %bitcast.74, ...), custom_call_target="tpu_custom_call" | custom-call | flops 13287555072 | bytes 9437184 | tf_op jit(solution)/shard_map/pallas_call | solution.py:239
  168.3 1.0 fusion.10
  169.3 0.6 fusion.24
  170.0 1.8 fusion.4
  171.9 4.7 %copy.42 = bf16[1024,3,512]{0,2,1:T(8,128)(2,1)} copy(bf16[1024,3,512]{2,0,1:T(8,128)(2,1)} %param.21) | data formatting | bytes 6291456 | tf_op args[5]
  176.6 125.3 %all-reduce.2.cloned.1.call-done = f32[48,1024]{1,0:T(8,128)} async-done(((f32[48,1024]{1,0:T(8,128)}), f32[48,1024]{1,0:T(8,128)}) %all-reduce.2.cloned.1.call-update) | async-done | bytes 196624 | tf_op jit(solution)/shard_map/psum | solution.py:378
  301.9 1.1 fusion.17
  303.2 3.0 convolution_convert_fusion
  306.8 0.4 fusion.23
  307.5 1.0 convolution_convert_fusion.2
  308.5 11.0 %reduce-scatter.2.cloned.1.call-done = bf16[48,512]{1,0:T(8,128)(2,1)} async-done(((bf16[48,1024]{1,0:T(8,128)(2,1)}), bf16[48,512]{1,0:T(8,128)(2,1)}) %reduce-scatter.2.cloned.1.call-update) | async-done | bytes 49168 | tf_op jit(solution)/shard_map/reduce_scatter | solution.py:397
  319.5 1.4 convert_add_fusion
  (56 shorter events, 3.3 us)
Async XLA Ops:
  7.2 162.1 %copy-start = (bf16[512,1024]{1,0:T(8,128)(2,1)S(1)}, bf16[512,1024]{1,0:T(8,128)(2,1)}, u32[]{:S(2)}) copy-start(bf16[512,1024]{1,0:T(8,128)(2,1)} %param.19) | copy-start | bytes 3145732
  7.2 294.7 %all-reduce.2.cloned.1.call-start = ((), (), s32[]{:S(2)}) async-start(), calls=%async_computation.1 | async-start | bytes 393216 | tf_op jit(solution)/shard_map/psum | solution.py:378
  7.2 8.9 %copy-start.3 = (s32[48]{0:T(128)S(1)}, s32[48]{0:T(128)}, u32[]{:S(2)}) copy-start(s32[48]{0:T(128)} %param.23) | copy-start | bytes 580
  7.2 9.2 %copy-start.4 = (s32[48]{0:T(128)S(1)}, s32[48]{0:T(128)}, u32[]{:S(2)}) copy-start(s32[48]{0:T(128)} %param.24) | copy-start | bytes 580
  10.7 14.4 %collective-permute-start = (bf16[320,1024]{1,0:T(8,128)(2,1)}, bf16[320,1024]{1,0:T(8,128)(2,1)}, u32[]{:S(2)}, u32[]{:S(2)}) collective-permute-start(bf16[320,1024]{1,0:T(8,128)(2,1)} %pad_maximum_fusion.1), channel_id=1, source_target_pairs={{0,2},{2,4},{4,6},{6,8},{8,10},{10,12},{12,14},{14,16},{16,18},{18... | collective-permute-start | bytes 1966088 | tf_op jit(solution)/shard_map/ppermute | solution.py:289
  14.8 10.3 %collective-permute-start.1 = (bf16[320,1024]{1,0:T(8,128)(2,1)}, bf16[320,1024]{1,0:T(8,128)(2,1)}, u32[]{:S(2)}, u32[]{:S(2)}) collective-permute-start(bf16[320,1024]{1,0:T(8,128)(2,1)} %pad_maximum_fusion.2), channel_id=1, source_target_pairs={{2,0},{4,2},{6,4},{8,6},{10,8},{12,10},{14,12},{16,14},{18,16},{20... | collective-permute-start | bytes 1966088 | tf_op jit(solution)/shard_map/ppermute | solution.py:290
  21.0 2.6 copy-start.5
  171.8 147.7 %reduce-scatter.2.cloned.1.call-start = ((), (), s32[]{:S(2)}) async-start(), calls=%async_computation.2 | async-start | bytes 147456 | tf_op jit(solution)/shard_map/reduce_scatter | solution.py:397
  171.9 131.4 %copy-start.2 = (f32[1024]{0:T(1024)S(1)}, f32[1024]{0:T(1024)}, u32[]{:S(2)}) copy-start(f32[1024]{0:T(1024)} %param.20) | copy-start | bytes 12292
  306.2 1.3 copy-start.1
Sparse Core Ops, SparseCore 0:
  171.9 129.9 all-reduce.1
  308.6 10.8 reduce-scatter.1

commit v2 on v1

--- a/solution.py
+++ b/solution.py
@@ -48,23 +48,15 @@
 
 def selections():
     strips = strip_tokens()
-    flat = [t for s in strips for t in s]
-    own = one_hot(flat, TOK)
-    out = [own]
-    for row_piece, col_piece in ((0, 2), (1, 3)):
-        where = {t: i for i, t in enumerate(strips[row_piece])}
-        cols = {t: STRIP + i for i, t in enumerate(strips[col_piece])}
-        rows = []
-        for number, strip in enumerate(strips):
-            same = OFFSETS[number][0] == OFFSETS[row_piece][0]
-            for t in strip:
-                if same:
-                    rows.append(where[t])
-                elif number == col_piece:
-                    rows.append(cols[t])
-                else:
-                    rows.append(-1)
-        out.append(one_hot(rows, 2 * STRIP))
+    out = [one_hot([t for s in strips for t in s], TOK)]
+    for piece in (0, 1):
+        where = {t: i for i, t in enumerate(strips[piece])}
+        for half in (0, 1):
+            rows = []
+            for number, strip in enumerate(strips):
+                same = OFFSETS[number][0] == OFFSETS[piece][0]
+                rows += [where[t] + half * STRIP if same else -1 for t in strip]
+            out.append(one_hot(rows, 2 * STRIP))
     return out
 
 
@@ -90,15 +82,17 @@
     tok_ref,
     halo_ref,
     gain_ref,
-    wq_ref,
-    wk_ref,
-    wv_ref,
+    wt_ref,
     sel_ref,
     selt_ref,
-    selp_ref,
-    selpt_ref,
-    seln_ref,
-    selnt_ref,
+    sel00_ref,
+    selt00_ref,
+    sel01_ref,
+    selt01_ref,
+    sel10_ref,
+    selt10_ref,
+    sel11_ref,
+    selt11_ref,
     mixed_ref,
     tsum_ref,
     msum_ref,
@@ -125,36 +119,41 @@
     @pl.when(step == 0)
     def _():
         qz_s[...] = jnp.zeros_like(qz_s)
-        gain = gain_ref[...]
-        normed = normalize(halo_ref[...].astype(jnp.float32), gain)
-        half = (HALO_WIN + 1) * STRIP
-        for side, sel, selt, first in (
-            (0, selp_ref, selpt_ref, 0),
-            (1, seln_ref, selnt_ref, HALO_WIN + win_count),
+        normed = normalize(halo_ref[...].astype(jnp.float32), gain_ref[...])
+        kvt = nt_dot(wt_ref[width:], normed).astype(jnp.bfloat16)
+        k = kvt[:width].T
+        half = SIDE_LANES
+        for side, tables, first, edge in (
+            (0, ((sel00_ref, selt00_ref), (sel01_ref, selt01_ref)), 0, HALO_WIN - 1),
+            (
+                1,
+                ((sel10_ref, selt10_ref), (sel11_ref, selt11_ref)),
+                HALO_WIN + win_count,
+                HALO_WIN + win_count,
+            ),
         ):
-            base = side * half
             for i in range(HALO_WIN):
-                piece = jnp.concatenate(
-                    [
-                        normed[base + i * STRIP : base + (i + 1) * STRIP],
-                        normed[base + HALO_WIN * STRIP : base + half],
-                    ],
-                    axis=0,
+                lo = side * half + (i // 2) * 128
+                sel, selt = tables[i % 2]
+                put_side(
+                    first + i, k[lo : lo + 128], kvt[width:, lo : lo + 128], sel[...], selt[...]
                 )
-                k = nn_dot(piece, wk_ref[...]).astype(jnp.bfloat16)
-                vt = nt_dot(wv_ref[...], piece).astype(jnp.bfloat16)
-                put_side(first + i, k, vt, sel[...], selt[...])
+            lo = side * half + 2 * 128
+            for g in range(groups):
+                ks_s[edge, g, 2 * STRIP : 4 * STRIP] = k[lo : lo + 128, g * 128 : (g + 1) * 128]
+            vs_s[edge, :, 128:256] = kvt[width:, lo : lo + 128]
 
     @pl.when(step < win_count)
     def _():
         values = tok_ref[...].astype(jnp.float32)
         tsum_ref[0] = jnp.sum(values, axis=0, keepdims=True)
         normed = normalize(values, gain_ref[...])
-        qt_s[step] = nt_dot(wq_ref[...], normed).astype(jnp.bfloat16)
-        k = nn_dot(normed, wk_ref[...]).astype(jnp.bfloat16)
+        qkvt = nt_dot(wt_ref[...], normed).astype(jnp.bfloat16)
+        qt_s[step] = qkvt[:width]
+        k = qkvt[width : 2 * width].T
         for g in range(groups):
             ko_s[step, g] = k[:, g * 128 : (g + 1) * 128]
-        vt = nt_dot(wv_ref[...], normed).astype(jnp.bfloat16)
+        vt = qkvt[2 * width :]
         vo_s[step] = vt
         put_side(step + HALO_WIN, k, vt, sel_ref[...], selt_ref[...])
 
@@ -204,12 +203,12 @@
                 top = jnp.max(scaled, axis=0, keepdims=True)
                 weights = jnp.exp2(scaled - top)
                 inverse = 1.0 / jnp.sum(weights, axis=0, keepdims=True)
-                probs = (weights * inverse).astype(jnp.bfloat16)
                 row = pl.multiple_of(head * HDIM, HDIM)
-                ot_s[pl.ds(row, HDIM), :] = nn_dot(ve_s[pl.ds(row, HDIM), :KEYS], probs)
+                summed = nn_dot(ve_s[pl.ds(row, HDIM), :KEYS], weights.astype(jnp.bfloat16))
+                ot_s[pl.ds(row, HDIM), :] = summed * inverse
             return carry
 
-        lax.fori_loop(0, groups, group, 0)
+        lax.fori_loop(0, groups, group, 0, unroll=2)
         mixed = ot_s[...].T.astype(jnp.bfloat16)
         mixed_ref[...] = mixed
         msum_ref[0] = jnp.sum(mixed.astype(jnp.float32), axis=0, keepdims=True)
@@ -219,7 +218,7 @@
     win_count = tokens.shape[0] // TOK
     width = weight.shape[2]
     groups = width // 128
-    wq, wk, wv = weight[:, 0].T, weight[:, 1], weight[:, 2].T
+    wt = weight.reshape(D, 3 * width).T
     tables = [t for pair in selections() for t in pair]
 
     def whole(array):
@@ -233,7 +232,7 @@
     def second(i, *_):
         return jnp.maximum(i - win_count, 0)
 
-    fixed = [halo, gain.reshape(1, D), wq, wk, wv] + tables
+    fixed = [halo, gain.reshape(1, D), wt] + tables
     slots_n = win_count + 2 * HALO_WIN
     bf = jnp.bfloat16
     return pl.pallas_call(
@@ -288,7 +287,102 @@
     )
     before = lax.ppermute(tail, "pack", [(i, i + 1) for i in range(count - 1)])
     after = lax.ppermute(head, "pack", [(i + 1, i) for i in range(count - 1)])
-    return jnp.concatenate([before, after])
+    blank = jnp.zeros((STRIP, D), tokens.dtype)
+    outer = HALO_WIN * STRIP
+    return jnp.concatenate([before, blank, after[:outer], blank, after[outer:]])
+
+
+def sum_kernel(count, heads, x_ref, out_ref, land, acc, full, send_sem, recv_sem):
+    me = lax.axis_index("pack") * heads + lax.axis_index("head")
+
+    def device(k):
+        other = lax.rem(me + k, count)
+        return other, {"pack": lax.div(other, heads), "head": lax.rem(other, heads)}
+
+    barrier = pltpu.get_barrier_semaphore()
+
+    @pl.loop(1, count)
+    def _(k):
+        pl.semaphore_signal(
+            barrier, inc=1, device_id=device(k)[1], device_id_type=pl.DeviceIdType.MESH
+        )
+
+    pl.semaphore_wait(barrier, count - 1)
+
+    def copy(k, phase):
+        other, where = device(k)
+        return pltpu.make_async_remote_copy(
+            src_ref=acc if phase else x_ref.at[other],
+            dst_ref=full.at[me] if phase else land.at[k],
+            send_sem=send_sem.at[phase, k],
+            recv_sem=recv_sem.at[phase, k],
+            device_id=where,
+            device_id_type=pl.DeviceIdType.MESH,
+        )
+
+    for phase in (0, 1):
+
+        @pl.loop(1, count)
+        def _(k):
+            copy(k, phase).start()
+
+        if phase:
+            full[me] = acc[...]
+        else:
+            land[0] = x_ref[me]
+
+        @pl.loop(1, count)
+        def _(k):
+            copy(k, phase).wait_recv()
+
+        if phase:
+            out_ref[...] = full[...]
+        else:
+            acc[...] = jnp.sum(land[...], axis=0)
+
+    @pl.loop(1, count)
+    def _(k):
+        copy(k, 0).wait_send()
+        copy(k, 1).wait_send()
+
+
+def sum_over_devices(values):
+    heads = lax.axis_size("head")
+    count = lax.axis_size("pack") * heads
+    rows = values.size // (count * 128)
+    shape = (count, rows, 128)
+    total = pl.pallas_call(
+        lambda *refs: sum_kernel(count, heads, *refs),
+        out_shape=jax.ShapeDtypeStruct(shape, jnp.float32),
+        in_specs=[pl.BlockSpec(memory_space=pltpu.VMEM)],
+        out_specs=pl.BlockSpec(memory_space=pltpu.VMEM),
+        scratch_shapes=[
+            pltpu.VMEM(shape, jnp.float32),
+            pltpu.VMEM(shape[1:], jnp.float32),
+            pltpu.VMEM(shape, jnp.float32),
+            pltpu.SemaphoreType.DMA((2, count)),
+            pltpu.SemaphoreType.DMA((2, count)),
+        ],
+        compiler_params=pltpu.CompilerParams(collective_id=0, has_side_effects=True),
+    )(values.reshape(shape))
+    return total.reshape(values.shape)
+
+
+def keep_share(values):
+    heads = lax.axis_size("head")
+    me = lax.axis_index("head")
+    columns = values.shape[1] // heads
+    rounded = values.astype(jnp.bfloat16)
+
+    def part(k):
+        start = lax.rem(me + k, heads) * columns
+        return lax.dynamic_slice_in_dim(rounded, start, columns, 1)
+
+    total = part(0).astype(jnp.float32)
+    for k in range(1, heads):
+        pairs = [(i, (i + k) % heads) for i in range(heads)]
+        total = total + lax.ppermute(part(k), "head", pairs).astype(jnp.float32)
+    return total
 
 
 def layer_norm(values, gain):
@@ -375,7 +469,7 @@
     projected = jnp.dot(page_mixed, attn_proj.astype(jnp.float32), precision=highest)
     share = jnp.where(lax.axis_index("head") == 0, 1.0, 0.0)
     counts = TOK * page_windows.astype(jnp.float32)
-    total = lax.psum(page_tokens * share + projected, ("pack", "head"))
+    total = sum_over_devices(page_tokens * share + projected)
     pooled = total / counts[:, None]
     page_count = page_windows.shape[0]
     page_normed = layer_norm(pooled, page_gain)
@@ -394,9 +488,7 @@
         local_heads,
     )
     branch = jnp.dot(context, page_proj, preferred_element_type=jnp.float32)
-    my_share = lax.psum_scatter(
-        branch.astype(jnp.bfloat16), "head", scatter_dimension=1, tiled=True
-    ).astype(jnp.float32)
+    my_share = keep_share(branch)
     column_start = lax.axis_index("head") * my_share.shape[1]
     page_out = lax.dynamic_slice_in_dim(pooled, column_start, my_share.shape[1], 1) + my_share
     return (mixed, page_out)

time: 328 us -> 188 us (0.57)
  waiting for transfers between devices: 136 us -> 3.37 us
  between operations: 14.3 us -> 1.01 us
  local copies, waits for them, and re-layouts: 14.5 us -> 19.1 us
    psum x1 -> x0, waiting for transfers between devices: 125 us -> none  [shards(): total = lax.psum(page_tokens * share + projected, ('pack', 'head'))]
    pallas_call x0 -> x1, Pallas kernels: none -> 21.5 us  [sum_over_devices(): pl.pallas_call(lambda *refs: sum_kernel(count, heads, *refs), out_shape=j...]
    pallas_call x1, Pallas kernels: 141 us -> 121 us  [window_layer(): pl.pallas_call(lambda *refs: window_kernel(win_count, width, *refs), out_...]
    reduce_scatter x1 -> x0, waiting for transfers between devices: 11 us -> none  [shards(): lax.psum_scatter(branch.astype(jnp.bfloat16), 'head', scatter_dimension=1...]
    unnamed x15 -> x22, local copies, waits for them, and re-layouts: 7.36 us -> 12.3 us
    ppermute x0 -> x1, waiting for transfers between devices: none -> 3.36 us  [keep_share(): total = total + lax.ppermute(part(k), 'head', pairs).astype(jnp.float32)]
  transfers between devices with their start and end apart: 4 -> 3, of which waited for: 2 -> 1; matrix products, arithmetic and copies ran while one was open for 4% -> 9% of each run, Pallas kernels for 0% -> 0%
where the time goes in v2:
time: 188 us; the launch traced here: 187 us
  Pallas kernels  143 us (76%)
  local copies, waits for them, and re-layouts  19.1 us (10%)
  other arithmetic  8.28 us (4%)
  matrix products  6.93 us (4%)
  starting transfers between devices  5.94 us (3%)
  waiting for transfers between devices  3.37 us (2%)
    pallas_call x1, Pallas kernels, window_layer(): pl.pallas_call(lambda *refs: window_kernel(win_count, width, *refs), out_...  121 us
    pallas_call x1, Pallas kernels, sum_over_devices(): pl.pallas_call(lambda *refs: sum_kernel(count, heads, *refs), out_shape=j...  21.5 us
    unnamed x22, local copies, waits for them, and re-layouts  12.3 us
    ppermute x1, starting transfers between devices, halo_tokens(): before = lax.ppermute(tail, 'pack', [(i, i + 1) for i in range(count - 1)])  3.89 us
  transfers between devices with their start and end apart: 3, of which 1 were waited for; matrix products, arithmetic and copies ran while one was open for 9% of the time, Pallas kernels for 0%

profile of v2, /device:TPU:0, one launch (start us, length us, event | category | flops | bytes accessed | tf_op | source)
XLA Modules:
  0.0 187.4 jit_solution(12289005909022079757)
XLA Ops:
  0.6 1.4 fusion.17
  2.0 1.1 fusion.18
  3.3 1.3 collective-permute-start.1
  4.6 0.7 reshape_squeeze.6
  5.2 0.9 pad_maximum_fusion
  6.2 3.9 %collective-permute-start = (bf16[320,1024]{1,0:T(8,128)(2,1)S(1)}, bf16[320,1024]{1,0:T(8,128)(2,1)}, u32[]{:S(2)}, u32[]{:S(2)}) collective-permute-start(bf16[320,1024]{1,0:T(8,128)(2,1)S(1)} %pad_maximum_fusion), channel_id=1, source_target_pairs={{0,2},{2,4},{4,6},{6,8},{8,10},{10,12},{12,14},{14,16},{16,18},{18... | collective-permute-start | bytes 1966088 | tf_op jit(solution)/shard_map/ppermute | solution.py:288
  10.4 0.9 select_reduce_fusion.2
  13.0 4.7 %copy.42 = bf16[1024,3,512]{0,2,1:T(8,128)(2,1)} copy(bf16[1024,3,512]{2,0,1:T(8,128)(2,1)} %param.22) | data formatting | bytes 6291456 | tf_op args[2]
  18.0 4.7 %copy.43 = bf16[1024,3,512]{0,2,1:T(8,128)(2,1)} copy(bf16[1024,3,512]{2,0,1:T(8,128)(2,1)} %param.25) | data formatting | bytes 6291456 | tf_op args[5]
  24.1 1.1 constant_dynamic-update-slice_fusion
  25.4 1.1 copy-done.3
  26.5 121.3 %shard_map.203 = (bf16[3072,512]{1,0:T(8,128)(2,1)}, f32[12,1,1024]{2,1,0:T(1,128)}, f32[12,1,512]{2,1,0:T(1,128)}) custom-call(s32[96]{0:T(128)} %add_select_fusion.refs_0_, f32[96]{0:T(128)} %get-tuple-element.11.refs_1_, bf16[3072,1024]{1,0:T(8,128)(2,1)} %refs_2_.1, bf16[768,1024]{1,0:T(8,128)(2,1)} %copy-done.3, f32[1,1024]{1,0:T(1,128)} %bitcast.69, ...), custom_call_target="tpu_custom_call" | custom-call | flops 13287555072 | bytes 9437184 | tf_op jit(solution)/shard_map/pallas_call | solution.py:238
  147.8 1.0 fusion.8
  148.8 0.6 fusion.21
  149.5 1.2 fusion.4
  150.6 0.8 reshape.281.refs_0_
  151.4 21.5 %shard_map.204 = f32[32,12,128]{2,1,0:T(8,128)} custom-call(f32[32,12,128]{2,1,0:T(8,128)} %reshape.281.refs_0_), custom_call_target="tpu_custom_call" | custom-call | tf_op jit(solution)/shard_map/pallas_call | solution.py:354
  172.9 1.2 fusion.15
  174.4 1.3 multiply_reduce_fusion
  176.0 1.2 multiply_convert_fusion
  177.4 2.9 %convolution_convert_fusion = bf16[48,1536]{1,0:T(8,128)(2,1)S(1)} fusion(bf16[48,1024]{1,0:T(8,128)(2,1)S(1)} %convert_element_type.41, bf16[1024,1536]{0,1:T(8,128)(2,1)} %bitcast.56), kind=kOutput, calls=%fused_computation.1 | convolution fusion | flops 151068672 | bytes 3391488 | tf_op jit(solution)/shard_map/dot_general | solution.py:476
  182.5 0.8 collective-permute-start.2
  183.3 3.4 %collective-permute-done.2 = bf16[48,512]{1,0:T(8,128)(2,1)S(1)} collective-permute-done((bf16[48,512]{1,0:T(8,128)(2,1)S(1)}, bf16[48,512]{1,0:T(8,128)(2,1)S(1)}, u32[]{:S(2)}, u32[]{:S(2)}) %collective-permute-start.2) | collective-permute-done | bytes 49184 | tf_op jit(solution)/shard_map/ppermute | solution.py:384
  186.7 0.7 fusion.5
  (76 shorter events, 6.7 us)
Async XLA Ops:
  0.6 148.2 %copy-start = (bf16[512,1024]{1,0:T(8,128)(2,1)S(1)}, bf16[512,1024]{1,0:T(8,128)(2,1)}, u32[]{:S(2)}) copy-start(bf16[512,1024]{1,0:T(8,128)(2,1)} %param.23) | copy-start | bytes 3145732
  3.2 6.9 %copy-start.5 = (s32[48]{0:T(128)S(1)}, s32[48]{0:T(128)}, u32[]{:S(2)}) copy-start(s32[48]{0:T(128)} %param.27) | copy-start | bytes 580
  3.3 22.0 %collective-permute-start.1 = (bf16[320,1024]{1,0:T(8,128)(2,1)S(1)}, bf16[320,1024]{1,0:T(8,128)(2,1)S(1)}, u32[]{:S(2)}, u32[]{:S(2)}) collective-permute-start(bf16[320,1024]{1,0:T(8,128)(2,1)S(1)} %pad_maximum_fusion.1), channel_id=1, source_target_pairs={{2,0},{4,2},{6,4},{8,6},{10,8},{12,10},{14,12},{16,14},{18,16},{20... | collective-permute-start | bytes 1966088 | tf_op jit(solution)/shard_map/ppermute | solution.py:289
  6.2 17.9 %collective-permute-start = (bf16[320,1024]{1,0:T(8,128)(2,1)S(1)}, bf16[320,1024]{1,0:T(8,128)(2,1)}, u32[]{:S(2)}, u32[]{:S(2)}) collective-permute-start(bf16[320,1024]{1,0:T(8,128)(2,1)S(1)} %pad_maximum_fusion), channel_id=1, source_target_pairs={{0,2},{2,4},{4,6},{6,8},{8,10},{10,12},{12,14},{14,16},{16,18},{18... | collective-permute-start | bytes 1966088 | tf_op jit(solution)/shard_map/ppermute | solution.py:288
  13.0 4.9 %copy-start.4 = (f32[1024]{0:T(1024)S(1)}, f32[1024]{0:T(1024)}, u32[]{:S(2)}) copy-start(f32[1024]{0:T(1024)} %param.24) | copy-start | bytes 12292
  17.9 4.7 %copy-start.7 = (s32[12]{0:T(128)S(1)}, s32[12]{0:T(128)}, u32[]{:S(2)}) copy-start(s32[12]{0:T(128)} %param.29) | copy-start | bytes 148
  17.9 5.5 %copy-start.6 = (s32[96]{0:T(128)S(1)}, s32[96]{0:T(128)}, u32[]{:S(2)}) copy-start(s32[96]{0:T(128)} %broadcast_in_dim.29) | copy-start | bytes 1156
  25.3 1.1 copy-start.3
  180.9 1.2 copy-start.2
  181.4 1.8 copy-start.1
  182.5 4.2 %collective-permute-start.2 = (bf16[48,512]{1,0:T(8,128)(2,1)S(1)}, bf16[48,512]{1,0:T(8,128)(2,1)S(1)}, u32[]{:S(2)}, u32[]{:S(2)}) collective-permute-start(bf16[48,512]{1,0:T(8,128)(2,1)S(1)} %constant_dynamic-slice_fusion), channel_id=1, source_target_pairs={{0,1},{1,0},{2,3},{3,2},{4,5},{5,4},{6,7},{7,6},{8,9},{9,8},{10,11... | collective-permute-start | bytes 147464 | tf_op jit(solution)/shard_map/ppermute | solution.py:384

commit v3 on v2

--- a/solution.py
+++ b/solution.py
@@ -292,76 +292,100 @@
     return jnp.concatenate([before, blank, after[:outer], blank, after[outer:]])
 
 
-def sum_kernel(count, heads, x_ref, out_ref, land, acc, full, send_sem, recv_sem):
-    me = lax.axis_index("pack") * heads + lax.axis_index("head")
-
-    def device(k):
-        other = lax.rem(me + k, count)
-        return other, {"pack": lax.div(other, heads), "head": lax.rem(other, heads)}
+def sum_kernel(wide, near_n, heads, x_ref, out_ref, land1, mid, land2, acc, row, full, sends, recvs):
+    per_near = near_n // heads
+    pack = lax.axis_index("pack")
+    a = lax.div(pack, per_near)
+    b = lax.rem(pack, per_near) * heads + lax.axis_index("head")
+
+    def beside(k):
+        other = lax.rem(b + k, near_n)
+        where = {"pack": a * per_near + lax.div(other, heads), "head": lax.rem(other, heads)}
+        return other, where
+
+    def across(k):
+        other = lax.rem(a + k, wide)
+        where = {"pack": other * per_near + lax.rem(pack, per_near), "head": lax.axis_index("head")}
+        return other, where
 
     barrier = pltpu.get_barrier_semaphore()
-
-    @pl.loop(1, count)
-    def _(k):
-        pl.semaphore_signal(
-            barrier, inc=1, device_id=device(k)[1], device_id_type=pl.DeviceIdType.MESH
-        )
-
-    pl.semaphore_wait(barrier, count - 1)
-
-    def copy(k, phase):
-        other, where = device(k)
+    for side, size in ((beside, near_n), (across, wide)):
+
+        @pl.loop(1, size)
+        def _(k):
+            pl.semaphore_signal(
+                barrier, inc=1, device_id=side(k)[1], device_id_type=pl.DeviceIdType.MESH
+            )
+
+    pl.semaphore_wait(barrier, near_n + wide - 2)
+
+    def copy(k, stage):
+        other, where = beside(k) if stage in (0, 3) else across(k)
+        source = (x_ref.at[other], mid.at[other], acc, row)[stage]
+        target = (land1.at[k], land2.at[k], row.at[a], full.at[b])[stage]
         return pltpu.make_async_remote_copy(
-            src_ref=acc if phase else x_ref.at[other],
-            dst_ref=full.at[me] if phase else land.at[k],
-            send_sem=send_sem.at[phase, k],
-            recv_sem=recv_sem.at[phase, k],
+            src_ref=source,
+            dst_ref=target,
+            send_sem=sends.at[stage, k],
+            recv_sem=recvs.at[stage, k],
             device_id=where,
             device_id_type=pl.DeviceIdType.MESH,
         )
 
-    for phase in (0, 1):
-
-        @pl.loop(1, count)
+    for stage, size in ((0, near_n), (1, wide), (2, wide), (3, near_n)):
+
+        @pl.loop(1, size)
         def _(k):
-            copy(k, phase).start()
-
-        if phase:
-            full[me] = acc[...]
+            copy(k, stage).start()
+
+        if stage == 0:
+            land1[0] = x_ref[b]
+        elif stage == 1:
+            land2[0] = mid[a]
+        elif stage == 2:
+            row[a] = acc[...]
         else:
-            land[0] = x_ref[me]
-
-        @pl.loop(1, count)
+            full[b] = row[...]
+
+        @pl.loop(1, size)
         def _(k):
-            copy(k, phase).wait_recv()
-
-        if phase:
+            copy(k, stage).wait_recv()
+
+        if stage == 0:
+            mid[...] = jnp.sum(land1[...], axis=0)
+        elif stage == 1:
+            acc[...] = jnp.sum(land2[...], axis=0)
+        elif stage == 3:
             out_ref[...] = full[...]
-        else:
-            acc[...] = jnp.sum(land[...], axis=0)
-
-    @pl.loop(1, count)
-    def _(k):
-        copy(k, 0).wait_send()
-        copy(k, 1).wait_send()
+
+    for stage, size in ((0, near_n), (1, wide), (2, wide), (3, near_n)):
+
+        @pl.loop(1, size)
+        def _(k):
+            copy(k, stage).wait_send()
 
 
 def sum_over_devices(values):
     heads = lax.axis_size("head")
-    count = lax.axis_size("pack") * heads
-    rows = values.size // (count * 128)
-    shape = (count, rows, 128)
+    packs = lax.axis_size("pack")
+    near_n = heads * (2 if packs % 2 == 0 else 1)
+    wide = packs * heads // near_n
+    rows = values.size // (packs * heads * 128)
+    shape = (near_n, wide, rows, 128)
     total = pl.pallas_call(
-        lambda *refs: sum_kernel(count, heads, *refs),
+        lambda *refs: sum_kernel(wide, near_n, heads, *refs),
         out_shape=jax.ShapeDtypeStruct(shape, jnp.float32),
         in_specs=[pl.BlockSpec(memory_space=pltpu.VMEM)],
         out_specs=pl.BlockSpec(memory_space=pltpu.VMEM),
         scratch_shapes=[
             pltpu.VMEM(shape, jnp.float32),
             pltpu.VMEM(shape[1:], jnp.float32),
+            pltpu.VMEM(shape[1:], jnp.float32),
+            pltpu.VMEM(shape[2:], jnp.float32),
+            pltpu.VMEM(shape[1:], jnp.float32),
             pltpu.VMEM(shape, jnp.float32),
-            pltpu.SemaphoreType.DMA((2, count)),
-            pltpu.SemaphoreType.DMA((2, count)),
+            pltpu.SemaphoreType.DMA((4, max(wide, near_n))),
+            pltpu.SemaphoreType.DMA((4, max(wide, near_n))),
         ],
         compiler_params=pltpu.CompilerParams(collective_id=0, has_side_effects=True),
     )(values.reshape(shape))

time: 188 us -> 191 us (1.016)
  Pallas kernels: 143 us -> 145 us
    pallas_call x1, Pallas kernels: 21.5 us -> 24.1 us  [sum_over_devices(): pl.pallas_call(lambda *refs: sum_kernel(wide, near_n, heads, *refs), out_...]
where the time goes in v3:
time: 191 us; the launch traced here: 190 us
  Pallas kernels  145 us (76%)
  local copies, waits for them, and re-layouts  19.1 us (10%)
  other arithmetic  8.33 us (4%)
  matrix products  6.93 us (4%)
  starting transfers between devices  6.3 us (3%)
  waiting for transfers between devices  3 us (2%)
    pallas_call x1, Pallas kernels, window_layer(): pl.pallas_call(lambda *refs: window_kernel(win_count, width, *refs), out_...  121 us
    pallas_call x1, Pallas kernels, sum_over_devices(): pl.pallas_call(lambda *refs: sum_kernel(wide, near_n, heads, *refs), out_...  24.1 us
    unnamed x22, local copies, waits for them, and re-layouts  12.3 us
    ppermute x1, starting transfers between devices, halo_tokens(): before = lax.ppermute(tail, 'pack', [(i, i + 1) for i in range(count - 1)])  3.89 us
  transfers between devices with their start and end apart: 3, of which 1 were waited for; matrix products, arithmetic and copies ran while one was open for 9% of the time, Pallas kernels for 0%

profile of v3, /device:TPU:0, one launch (start us, length us, event | category | flops | bytes accessed | tf_op | source)
XLA Modules:
  0.0 190.0 jit_solution(5608119616128499579)
XLA Ops:
  0.6 1.4 fusion.17
  2.0 1.1 fusion.18
  3.3 1.3 collective-permute-start.1
  4.6 0.7 reshape_squeeze.6
  5.2 0.9 pad_maximum_fusion
  6.2 3.9 %collective-permute-start = (bf16[320,1024]{1,0:T(8,128)(2,1)S(1)}, bf16[320,1024]{1,0:T(8,128)(2,1)}, u32[]{:S(2)}, u32[]{:S(2)}) collective-permute-start(bf16[320,1024]{1,0:T(8,128)(2,1)S(1)} %pad_maximum_fusion), channel_id=1, source_target_pairs={{0,2},{2,4},{4,6},{6,8},{8,10},{10,12},{12,14},{14,16},{16,18},{18... | collective-permute-start | bytes 1966088 | tf_op jit(solution)/shard_map/ppermute | solution.py:288
  10.4 0.9 select_reduce_fusion.2
  13.0 4.7 %copy.42 = bf16[1024,3,512]{0,2,1:T(8,128)(2,1)} copy(bf16[1024,3,512]{2,0,1:T(8,128)(2,1)} %param.22) | data formatting | bytes 6291456 | tf_op args[2]
  18.0 4.7 %copy.43 = bf16[1024,3,512]{0,2,1:T(8,128)(2,1)} copy(bf16[1024,3,512]{2,0,1:T(8,128)(2,1)} %param.25) | data formatting | bytes 6291456 | tf_op args[5]
  24.1 1.1 constant_dynamic-update-slice_fusion
  25.4 1.1 copy-done.3
  26.5 121.3 %shard_map.203 = (bf16[3072,512]{1,0:T(8,128)(2,1)}, f32[12,1,1024]{2,1,0:T(1,128)}, f32[12,1,512]{2,1,0:T(1,128)}) custom-call(s32[96]{0:T(128)} %add_select_fusion.refs_0_, f32[96]{0:T(128)} %get-tuple-element.11.refs_1_, bf16[3072,1024]{1,0:T(8,128)(2,1)} %refs_2_.1, bf16[768,1024]{1,0:T(8,128)(2,1)} %copy-done.3, f32[1,1024]{1,0:T(1,128)} %bitcast.69, ...), custom_call_target="tpu_custom_call" | custom-call | flops 13287555072 | bytes 9437184 | tf_op jit(solution)/shard_map/pallas_call | solution.py:238
  147.8 1.0 fusion.8
  148.8 0.6 fusion.21
  149.5 1.2 fusion.4
  150.6 0.8 reshape.281.refs_0_
  151.4 24.1 %shard_map.204 = f32[4,8,12,128]{3,2,1,0:T(8,128)} custom-call(f32[4,8,12,128]{3,2,1,0:T(8,128)} %reshape.281.refs_0_), custom_call_target="tpu_custom_call" | custom-call | tf_op jit(solution)/shard_map/pallas_call | solution.py:375
  175.4 1.2 fusion.15
  177.0 1.3 multiply_reduce_fusion
  178.7 1.2 multiply_convert_fusion
  180.1 2.9 %convolution_convert_fusion = bf16[48,1536]{1,0:T(8,128)(2,1)S(1)} fusion(bf16[48,1024]{1,0:T(8,128)(2,1)S(1)} %convert_element_type.41, bf16[1024,1536]{0,1:T(8,128)(2,1)} %bitcast.56), kind=kOutput, calls=%fused_computation.1 | convolution fusion | flops 151068672 | bytes 3391488 | tf_op jit(solution)/shard_map/dot_general | solution.py:500
  185.1 1.1 collective-permute-start.2
  186.3 3.0 %collective-permute-done.2 = bf16[48,512]{1,0:T(8,128)(2,1)S(1)} collective-permute-done((bf16[48,512]{1,0:T(8,128)(2,1)S(1)}, bf16[48,512]{1,0:T(8,128)(2,1)S(1)}, u32[]{:S(2)}, u32[]{:S(2)}) %collective-permute-start.2) | collective-permute-done | bytes 49184 | tf_op jit(solution)/shard_map/ppermute | solution.py:408
  189.3 0.7 fusion.5
  (76 shorter events, 6.7 us)
Async XLA Ops:
  0.6 148.2 %copy-start = (bf16[512,1024]{1,0:T(8,128)(2,1)S(1)}, bf16[512,1024]{1,0:T(8,128)(2,1)}, u32[]{:S(2)}) copy-start(bf16[512,1024]{1,0:T(8,128)(2,1)} %param.23) | copy-start | bytes 3145732
  3.2 6.9 %copy-start.5 = (s32[48]{0:T(128)S(1)}, s32[48]{0:T(128)}, u32[]{:S(2)}) copy-start(s32[48]{0:T(128)} %param.27) | copy-start | bytes 580
  3.3 22.0 %collective-permute-start.1 = (bf16[320,1024]{1,0:T(8,128)(2,1)S(1)}, bf16[320,1024]{1,0:T(8,128)(2,1)S(1)}, u32[]{:S(2)}, u32[]{:S(2)}) collective-permute-start(bf16[320,1024]{1,0:T(8,128)(2,1)S(1)} %pad_maximum_fusion.1), channel_id=1, source_target_pairs={{2,0},{4,2},{6,4},{8,6},{10,8},{12,10},{14,12},{16,14},{18,16},{20... | collective-permute-start | bytes 1966088 | tf_op jit(solution)/shard_map/ppermute | solution.py:289
  6.2 17.9 %collective-permute-start = (bf16[320,1024]{1,0:T(8,128)(2,1)S(1)}, bf16[320,1024]{1,0:T(8,128)(2,1)}, u32[]{:S(2)}, u32[]{:S(2)}) collective-permute-start(bf16[320,1024]{1,0:T(8,128)(2,1)S(1)} %pad_maximum_fusion), channel_id=1, source_target_pairs={{0,2},{2,4},{4,6},{6,8},{8,10},{10,12},{12,14},{14,16},{16,18},{18... | collective-permute-start | bytes 1966088 | tf_op jit(solution)/shard_map/ppermute | solution.py:288
  13.0 4.9 %copy-start.4 = (f32[1024]{0:T(1024)S(1)}, f32[1024]{0:T(1024)}, u32[]{:S(2)}) copy-start(f32[1024]{0:T(1024)} %param.24) | copy-start | bytes 12292
  17.9 4.7 %copy-start.7 = (s32[12]{0:T(128)S(1)}, s32[12]{0:T(128)}, u32[]{:S(2)}) copy-start(s32[12]{0:T(128)} %param.29) | copy-start | bytes 148
  17.9 5.5 %copy-start.6 = (s32[96]{0:T(128)S(1)}, s32[96]{0:T(128)}, u32[]{:S(2)}) copy-start(s32[96]{0:T(128)} %broadcast_in_dim.29) | copy-start | bytes 1156
  25.3 1.1 copy-start.3
  183.5 1.2 copy-start.2
  184.0 2.2 %copy-start.1 = (f32[4,8,12,128]{3,2,1,0:T(8,128)S(1)}, f32[4,8,12,128]{3,2,1,0:T(8,128)}, u32[]{:S(2)}) copy-start(f32[4,8,12,128]{3,2,1,0:T(8,128)} %shard_map.204) | copy-start | bytes 589828
  185.1 4.2 %collective-permute-start.2 = (bf16[48,512]{1,0:T(8,128)(2,1)S(1)}, bf16[48,512]{1,0:T(8,128)(2,1)S(1)}, u32[]{:S(2)}, u32[]{:S(2)}) collective-permute-start(bf16[48,512]{1,0:T(8,128)(2,1)S(1)} %constant_dynamic-slice_fusion), channel_id=1, source_target_pairs={{0,1},{1,0},{2,3},{3,2},{4,5},{5,4},{6,7},{7,6},{8,9},{9,8},{10,11... | collective-permute-start | bytes 147464 | tf_op jit(solution)/shard_map/ppermute | solution.py:408
